TPU v7x, 32 devices: a whole 2x2x4 slice. The times are simulated.
32 devices in a mesh: rows: 8 (over z, y), code: 4 (over x, core).
Axes of the slice: x: 2, y: 2, z: 4, core: 2. Of those that a mesh axis runs over, the one named last changes fastest.
Arguments:
- embedding_vectors: bfloat16 [3072, 256], P('rows'), may hold values from -45.3125 to 45.3125
- codebook: bfloat16 [65536, 256], P(('code', 'rows')), may hold values from -0.38125 to 0.38125
- weights: float32 [3072], P('rows'), may hold values from 0.6 to 4.2
Outputs:
- gradient: float32 [65536, 256], P(('code', 'rows'))
- load: float32 [65536], P(('code', 'rows'))
All inputs are finite; a program needn't handle non-finite values.
Results may differ from a plain program's by a relative error of at most 0.013.
Values may be sent and summed in bfloat16 or wider, within the bound.
No kernel may reach another device: no remote copies, remote signals or barrier semaphores. Data moves between devices by JAX's collectives and lax.ppermute only.
A program may use at most 128 MiB of HBM per device.

v0:
```python
import jax
import jax.numpy as jnp
from jax import lax
from jax.sharding import PartitionSpec as P

ITERS = 3
sharpness_factor = 2.0


def local(embedding_vectors, codebook, weights):
    code_devices = lax.axis_size("code")
    balance = embedding_vectors.shape[0] / (code_devices * codebook.shape[0])
    similarity_table = sharpness_factor * jnp.einsum(
        "nd,kd->nk",
        embedding_vectors,
        lax.all_gather(codebook, "rows", axis=0, tiled=True),
        preferred_element_type=jnp.float32,
    )
    row_peak = lax.pmax(jnp.max(similarity_table, axis=1), "code")
    power_term = jnp.exp(similarity_table - row_peak[:, None])

    def marginal_per_sample(col_scale):
        return lax.psum(jnp.dot(power_term, col_scale, precision=lax.Precision.HIGHEST), "code")

    col_scale = jnp.ones((power_term.shape[1],), jnp.float32)
    row_scale = weights / marginal_per_sample(col_scale)
    for iteration in range(ITERS):
        partial_cols = jnp.dot(row_scale, power_term, precision=lax.Precision.HIGHEST)
        col_scale = balance / lax.psum(partial_cols, "rows")
        row_scale = weights / marginal_per_sample(col_scale)
    transport_plan = power_term * row_scale[:, None] * col_scale[None, :]
    local_mass = jnp.sum(transport_plan, axis=0)
    partial_aggregates = jnp.einsum(
        "nk,nd->kd",
        transport_plan.astype(jnp.bfloat16),
        embedding_vectors,
        preferred_element_type=jnp.float32,
    )
    codeword_sums, code_mass = (
        lax.psum_scatter(partial_aggregates, "rows", scatter_dimension=0, tiled=True),
        lax.psum_scatter(local_mass, "rows", scatter_dimension=0, tiled=True),
    )
    gradient = (code_mass[:, None] * codebook.astype(jnp.float32) - codeword_sums) / balance
    return (gradient, code_mass / balance)


def solution(mesh):
    placed = (P("rows", None), P(("code", "rows"), None), P("rows"))
    return jax.shard_map(
        local,
        mesh=mesh,
        in_specs=placed,
        out_specs=(P(("code", "rows"), None), P(("code", "rows"))),
        check_vma=False,
    )
```

profile of v0, /device:TPU:0, one launch (start us, length us, event | category | flops | bytes accessed | tf_op | source)
XLA Modules:
  0.0 927.6 jit_solution(9325484149887483975)
XLA Ops:
  7.2 0.0 copy-start
  7.2 0.0 all-gather.2.cloned.1.call-start
  7.2 0.7 all-gather.2.cloned.1.call-update
  7.9 0.0 copy-start.2
  7.9 0.0 all-reduce.6.cloned.1.call-start
  8.0 129.8 %all-gather.2.cloned.1.call-done = bf16[16384,256]{1,0:T(8,128)(2,1)} async-done(((bf16[2048,256]{1,0:T(8,128)(2,1)}), bf16[16384,256]{1,0:T(8,128)(2,1)}) %all-gather.2.cloned.1.call-update) | async-done | bytes 8388624 | tf_op jit(solution)/shard_map/all_gather | solution.py:16
  137.8 0.0 copy-done
  137.8 15.2 %fusion.11 = (f32[384]{0:T(512)S(1)}, f32[384,16384]{1,0:T(8,128)}) fusion(bf16[384,256]{1,0:T(8,128)(2,1)S(1)} %copy-done, bf16[16384,256]{1,0:T(8,128)(2,1)} %all-gather.2.cloned.1.call-done), kind=kOutput, calls=%fused_computation.22 | convolution fusion | flops 3233807872 | bytes 33752576 | tf_op jit(solution)/shard_map/nd,kd->nk/dot_general | solution.py:13
  153.0 6.1 pmax.7
  159.1 26.1 %convolution_reduce_fusion.3 = f32[384]{0:T(512)S(1)} fusion(f32[384,16384]{1,0:T(8,128)} %get-tuple-element.5, f32[384]{0:T(512)S(1)} %pmax.7), kind=kOutput, calls=%fused_computation.12 | convolution fusion | flops 81788928 | bytes 25168896 | tf_op jit(solution)/shard_map/dot_general | solution.py:23
  185.2 6.6 psum.49
  191.8 0.0 copy-done.2
  191.8 18.6 %fusion.10 = f32[1,16384]{1,0:T(1,128)} fusion(f32[384,1]{0,1:T(1,128)S(1)} %reshape.10, f32[384,16384]{1,0:T(8,128)} %get-tuple-element.5, f32[384]{0:T(512)S(1)} %pmax.7), kind=kOutput, calls=%fused_computation.21 | convolution fusion | flops 81788928 | bytes 25234432 | tf_op jit(solution)/shard_map/dot_general | solution.py:28
  210.5 0.0 all-reduce.6.cloned.1.call-update
  210.5 0.0 all-reduce.8.cloned.1.call-start
  210.6 66.2 %all-reduce.6.cloned.1.call-done = f32[16384]{0:T(1024)} async-done(((f32[16384]{0:T(1024)}), f32[16384]{0:T(1024)}) %all-reduce.6.cloned.1.call-update) | async-done | bytes 65552 | tf_op jit(solution)/shard_map/psum | solution.py:29
  276.8 0.9 broadcast_divide_fusion.2
  277.6 26.2 %convolution_reduce_fusion.2 = f32[384]{0:T(512)S(1)} fusion(f32[16384,1]{0,1:T(1,128)S(1)} %bitcast.20, f32[384,16384]{1,0:T(8,128)} %get-tuple-element.5, f32[384]{0:T(512)S(1)} %pmax.7), kind=kOutput, calls=%fused_computation.11 | convolution fusion | flops 81788928 | bytes 25234432 | tf_op jit(solution)/shard_map/dot_general | solution.py:23
  303.8 5.8 psum.51
  309.7 18.6 %fusion.9 = f32[1,16384]{1,0:T(1,128)} fusion(f32[384,1]{0,1:T(1,128)S(1)} %reshape.14, f32[384,16384]{1,0:T(8,128)} %get-tuple-element.5, f32[384]{0:T(512)S(1)} %pmax.7), kind=kOutput, calls=%fused_computation.20 | convolution fusion | flops 81788928 | bytes 25234432 | tf_op jit(solution)/shard_map/dot_general | solution.py:28
  328.3 0.0 all-reduce.8.cloned.1.call-update
  328.3 0.0 all-reduce.10.cloned.1.call-start
  328.4 68.8 %all-reduce.8.cloned.1.call-done = f32[16384]{0:T(1024)} async-done(((f32[16384]{0:T(1024)}), f32[16384]{0:T(1024)}) %all-reduce.8.cloned.1.call-update) | async-done | bytes 65552 | tf_op jit(solution)/shard_map/psum | solution.py:29
  397.1 0.9 broadcast_divide_fusion.1
  398.0 26.2 %convolution_reduce_fusion.1 = f32[384]{0:T(512)S(1)} fusion(f32[16384,1]{0,1:T(1,128)S(1)} %bitcast.21, f32[384,16384]{1,0:T(8,128)} %get-tuple-element.5, f32[384]{0:T(512)S(1)} %pmax.7), kind=kOutput, calls=%fused_computation.10 | convolution fusion | flops 81788928 | bytes 25234432 | tf_op jit(solution)/shard_map/dot_general | solution.py:23
  424.2 5.9 psum.53
  430.1 18.6 %fusion.8 = f32[1,16384]{1,0:T(1,128)} fusion(f32[384,1]{0,1:T(1,128)S(1)} %reshape.18, f32[384,16384]{1,0:T(8,128)} %get-tuple-element.5, f32[384]{0:T(512)S(1)} %pmax.7), kind=kOutput, calls=%fused_computation.19 | convolution fusion | flops 81788928 | bytes 25234432 | tf_op jit(solution)/shard_map/dot_general | solution.py:28
  448.7 0.0 all-reduce.10.cloned.1.call-update
  448.7 0.0 all-reduce.12.cloned.1.call-start
  448.8 68.8 %all-reduce.10.cloned.1.call-done = f32[16384]{0:T(1024)} async-done(((f32[16384]{0:T(1024)}), f32[16384]{0:T(1024)}) %all-reduce.10.cloned.1.call-update) | async-done | bytes 65552 | tf_op jit(solution)/shard_map/psum | solution.py:29
  517.6 0.9 broadcast_divide_fusion
  518.4 26.2 %convolution_reduce_fusion = f32[384]{0:T(512)S(1)} fusion(f32[16384,1]{0,1:T(1,128)S(1)} %bitcast.16, f32[384,16384]{1,0:T(8,128)} %get-tuple-element.5, f32[384]{0:T(512)S(1)} %pmax.7), kind=kOutput, calls=%fused_computation.9 | convolution fusion | flops 81788928 | bytes 25234432 | tf_op jit(solution)/shard_map/dot_general | solution.py:23
  544.6 5.7 psum.55
  550.3 11.9 %fusion.1 = f32[16384]{0:T(1024)} fusion(f32[16384]{0:T(1024)S(1)} %broadcast_divide_fusion, f32[384]{0:T(512)S(1)} %div.39, f32[384,16384]{1,0:T(8,128)} %get-tuple-element.5, f32[384]{0:T(512)S(1)} %pmax.7), kind=kLoop, calls=%fused_computation.4 | loop fusion | flops 25149440 | bytes 25299968 | tf_op jit(solution)/shard_map/reduce_sum | solution.py:32
  562.2 0.0 all-reduce.12.cloned.1.call-update
  562.3 0.0 copy-start.3
  562.3 0.0 copy-start.1
  562.3 0.3 reduce-scatter.2.cloned.1.call-start
  562.6 14.9 %fusion.2 = f32[16384,256]{1,0:T(8,128)} fusion(bf16[384,256]{1,0:T(8,128)(2,1)S(1)} %copy-done, f32[16384]{0:T(1024)S(1)} %broadcast_divide_fusion, f32[384]{0:T(512)S(1)} %div.39, f32[384,16384]{1,0:T(8,128)} %get-tuple-element.5, f32[384]{0:T(512)S(1)} %pmax.7), kind=kOutput, calls=%fused_computation.5 | convolution fusion | flops 3246391296 | bytes 42208256 | tf_op jit(solution)/shard_map/nk,nd->kd/dot_general | solution.py:33
  577.5 0.0 reduce-scatter.2.cloned.1.call-update
  577.5 0.0 copy-done.3
  577.6 0.6 dynamic-slice
  578.8 52.3 %all-reduce.12.cloned.1.call-done = f32[16384]{0:T(1024)} async-done(((f32[16384]{0:T(1024)}), f32[16384]{0:T(1024)}) %all-reduce.12.cloned.1.call-update) | async-done | bytes 65552
  631.1 1.3 broadcast_multiply_fusion
  632.4 284.8 %reduce-scatter.2.cloned.1.call-done = f32[2048,256]{1,0:T(8,128)} async-done(((f32[16384,256]{1,0:T(8,128)}), f32[2048,256]{1,0:T(8,128)}) %reduce-scatter.2.cloned.1.call-update) | async-done | bytes 2097168 | tf_op jit(solution)/shard_map/reduce_scatter | solution.py:40
  917.2 0.0 copy-done.1
  917.2 3.3 subtract_multiply_fusion
  (7 shorter events, 0.0 us)
Async XLA Ops:
  7.2 130.6 %copy-start = (bf16[384,256]{1,0:T(8,128)(2,1)S(1)}, bf16[384,256]{1,0:T(8,128)(2,1)}, u32[]{:S(2)}) copy-start(bf16[384,256]{1,0:T(8,128)(2,1)} %param.3) | copy-start | bytes 589828
  7.2 130.6 %all-gather.2.cloned.1.call-start = ((), (), s32[]{:S(2)}) async-start(), calls=%async_computation.1 | async-start | bytes 9437184 | tf_op jit(solution)/shard_map/all_gather | solution.py:16
  7.9 183.9 %copy-start.2 = (f32[384]{0:T(512)S(1)}, f32[384]{0:T(512)}, u32[]{:S(2)}) copy-start(f32[384]{0:T(512)} %param.5) | copy-start | bytes 4612
  7.9 268.8 %all-reduce.6.cloned.1.call-start = ((), (), s32[]{:S(2)}) async-start(), calls=%async_computation.2 | async-start | bytes 131072 | tf_op jit(solution)/shard_map/psum | solution.py:29
  210.5 186.6 %all-reduce.8.cloned.1.call-start = ((), (), s32[]{:S(2)}) async-start(), calls=%async_computation.3 | async-start | bytes 131072 | tf_op jit(solution)/shard_map/psum | solution.py:29
  328.3 189.3 %all-reduce.10.cloned.1.call-start = ((), (), s32[]{:S(2)}) async-start(), calls=%async_computation.4 | async-start | bytes 131072 | tf_op jit(solution)/shard_map/psum | solution.py:29
  448.7 182.4 %all-reduce.12.cloned.1.call-start = ((), (), s32[]{:S(2)}) async-start(), calls=%async_computation.6 | async-start | bytes 131072
  562.3 15.3 %copy-start.3 = (u32[32]{0:T(128)S(1)}, u32[32]{0:T(128)}, u32[]{:S(2)}) copy-start(u32[32]{0:T(128)} %constant.17) | copy-start | bytes 388
  562.3 354.9 %copy-start.1 = (bf16[2048,256]{1,0:T(8,128)(2,1)S(1)}, bf16[2048,256]{1,0:T(8,128)(2,1)}, u32[]{:S(2)}) copy-start(bf16[2048,256]{1,0:T(8,128)(2,1)} %param.4) | copy-start | bytes 3145732
  562.3 354.9 %reduce-scatter.2.cloned.1.call-start = ((), (), s32[]{:S(2)}) async-start(), calls=%async_computation.5 | async-start | bytes 18874368 | tf_op jit(solution)/shard_map/reduce_scatter | solution.py:40
Sparse Core Ops, SparseCore 0:
  10.1 127.6 all-gather.1
  210.6 66.0 all-reduce.5
  328.4 68.6 all-reduce.7
  448.9 68.6 all-reduce.9
  562.4 68.6 all-reduce.11
  634.7 282.4 reduce-scatter.1
where the time goes:
time: 935 us; the launch traced here: 928 us
  waiting for transfers between devices  671 us (72%)
  matrix products  191 us (20%)
  blocking collectives  30.1 us (3%)
  other arithmetic  19.1 us (2%)
  between operations  15.1 us (2%)
    reduce_scatter x1, waiting for transfers between devices, local(): lax.psum_scatter(partial_aggregates, 'rows', scatter_dimension=0, tiled=T...  285 us
    psum x3, waiting for transfers between devices, local(): col_scale = balance / lax.psum(partial_cols, 'rows')  204 us
    all_gather x1, waiting for transfers between devices, local(): lax.all_gather(codebook, 'rows', axis=0, tiled=True)  130 us
    dot_general x4, matrix products, marginal_per_sample(): jnp.dot(power_term, col_scale, precision=lax.Precision.HIGHEST)  105 us
    dot_general x3, matrix products, local(): jnp.dot(row_scale, power_term, precision=lax.Precision.HIGHEST)  55.9 us
    unnamed x7, waiting for transfers between devices  53.1 us
    psum x4, blocking collectives, marginal_per_sample(): lax.psum(jnp.dot(power_term, col_scale, precision=lax.Precision.HIGHEST),...  24 us
  transfers between devices with their start and end apart: 6, of which 6 were waited for; matrix products, arithmetic and copies ran while one was open for 2% of the time, Pallas kernels for 0%

commit v1 on v0

--- a/solution.py
+++ b/solution.py
@@ -26,7 +26,7 @@
     row_scale = weights / marginal_per_sample(col_scale)
     for iteration in range(ITERS):
         partial_cols = jnp.dot(row_scale, power_term, precision=lax.Precision.HIGHEST)
-        col_scale = balance / lax.psum(partial_cols, "rows")
+        col_scale = balance / jnp.sum(lax.all_gather(partial_cols, "rows"), axis=0)
         row_scale = weights / marginal_per_sample(col_scale)
     transport_plan = power_term * row_scale[:, None] * col_scale[None, :]
     local_mass = jnp.sum(transport_plan, axis=0)

time: 935 us -> 819 us (0.88)
  waiting for transfers between devices: 671 us -> 466 us
  blocking collectives: 30.1 us -> 124 us
    psum x3 -> x0, waiting for transfers between devices: 204 us -> none  [local(): col_scale = balance / lax.psum(partial_cols, 'rows')]
    all_gather x0 -> x3, blocking collectives: none -> 94 us  [local(): col_scale = balance / jnp.sum(lax.all_gather(partial_cols, 'rows'), axis=0)]
    unnamed x7 -> x4, waiting for transfers between devices: 53.1 us -> 51 us
  transfers between devices with their start and end apart: 6 -> 3, of which waited for: 6 -> 3; matrix products, arithmetic and copies ran while one was open for 2% -> 2% of each run, Pallas kernels for 0% -> 0%
where the time goes in v1:
time: 819 us; the launch traced here: 812 us
  waiting for transfers between devices  466 us (57%)
  matrix products  189 us (23%)
  blocking collectives  124 us (15%)
  other arithmetic  17 us (2%)
  between operations  14.8 us (2%)
    reduce_scatter x1, waiting for transfers between devices, local(): lax.psum_scatter(partial_aggregates, 'rows', scatter_dimension=0, tiled=T...  285 us
    all_gather x1, waiting for transfers between devices, local(): lax.all_gather(codebook, 'rows', axis=0, tiled=True)  130 us
    dot_general x4, matrix products, marginal_per_sample(): jnp.dot(power_term, col_scale, precision=lax.Precision.HIGHEST)  105 us
    all_gather x3, blocking collectives, local(): col_scale = balance / jnp.sum(lax.all_gather(partial_cols, 'rows'), axis=0)  94 us
    dot_general x3, matrix products, local(): jnp.dot(row_scale, power_term, precision=lax.Precision.HIGHEST)  54 us
    unnamed x4, waiting for transfers between devices  51 us
    psum x4, blocking collectives, marginal_per_sample(): lax.psum(jnp.dot(power_term, col_scale, precision=lax.Precision.HIGHEST),...  24 us
  transfers between devices with their start and end apart: 3, of which 3 were waited for; matrix products, arithmetic and copies ran while one was open for 2% of the time, Pallas kernels for 0%

profile of v1, /device:TPU:0, one launch (start us, length us, event | category | flops | bytes accessed | tf_op | source)
XLA Modules:
  0.0 811.8 jit_solution(12716565624459927110)
XLA Ops:
  7.2 0.0 copy-start
  7.2 0.0 all-gather.5.cloned.1.call-start
  7.2 0.7 all-gather.5.cloned.1.call-update
  7.9 0.0 copy-start.2
  7.9 0.0 all-reduce.3.cloned.1.call-start
  8.0 129.8 %all-gather.5.cloned.1.call-done = bf16[16384,256]{1,0:T(8,128)(2,1)} async-done(((bf16[2048,256]{1,0:T(8,128)(2,1)}), bf16[16384,256]{1,0:T(8,128)(2,1)}) %all-gather.5.cloned.1.call-update) | async-done | bytes 8388624 | tf_op jit(solution)/shard_map/all_gather | solution.py:16
  137.8 0.0 copy-done
  137.8 15.2 %fusion.11 = (f32[384]{0:T(512)S(1)}, f32[384,16384]{1,0:T(8,128)}) fusion(bf16[384,256]{1,0:T(8,128)(2,1)S(1)} %copy-done, bf16[16384,256]{1,0:T(8,128)(2,1)} %all-gather.5.cloned.1.call-done), kind=kOutput, calls=%fused_computation.22 | convolution fusion | flops 3233807872 | bytes 33752576 | tf_op jit(solution)/shard_map/nd,kd->nk/dot_general | solution.py:13
  153.0 6.1 pmax.7
  159.1 26.1 %convolution_reduce_fusion.3 = f32[384]{0:T(512)S(1)} fusion(f32[384,16384]{1,0:T(8,128)} %get-tuple-element.5, f32[384]{0:T(512)S(1)} %pmax.7), kind=kOutput, calls=%fused_computation.12 | convolution fusion | flops 81788928 | bytes 25168896 | tf_op jit(solution)/shard_map/dot_general | solution.py:23
  185.2 6.6 psum.28
  191.8 0.0 copy-done.2
  191.8 18.0 %fusion.10 = f32[1,16384]{1,0:T(1,128)S(1)} fusion(f32[384,1]{0,1:T(1,128)S(1)} %reshape.15, f32[384,16384]{1,0:T(8,128)} %get-tuple-element.5, f32[384]{0:T(512)S(1)} %pmax.7), kind=kOutput, calls=%fused_computation.21 | convolution fusion | flops 81788928 | bytes 25234432 | tf_op jit(solution)/shard_map/dot_general | solution.py:28
  209.9 31.2 %all-gather = f32[131072]{0:T(1024)S(1)} all-gather(f32[16384]{0:T(1024)S(1)} %bitcast.17), channel_id=2, replica_groups=mesh['rows'=8,'code'=4] {'rows'}, dimensions={0}, use_global_device_ids=true | all-gather | bytes 589824 | tf_op jit(solution)/shard_map/all_gather | solution.py:29
  241.1 0.1 reshape.10
  241.2 0.1 reduce_sum.36
  241.4 26.2 %convolution_reduce_fusion.2 = f32[384]{0:T(512)S(1)} fusion(f32[16384,1]{0,1:T(1,128)S(1)} %bitcast.20, f32[384,16384]{1,0:T(8,128)} %get-tuple-element.5, f32[384]{0:T(512)S(1)} %pmax.7), kind=kOutput, calls=%fused_computation.11 | convolution fusion | flops 81788928 | bytes 25234432 | tf_op jit(solution)/shard_map/dot_general | solution.py:23
  267.6 5.8 psum.29
  273.4 18.0 %fusion.9 = f32[1,16384]{1,0:T(1,128)S(1)} fusion(f32[384,1]{0,1:T(1,128)S(1)} %reshape.19, f32[384,16384]{1,0:T(8,128)} %get-tuple-element.5, f32[384]{0:T(512)S(1)} %pmax.7), kind=kOutput, calls=%fused_computation.20 | convolution fusion | flops 81788928 | bytes 25234432 | tf_op jit(solution)/shard_map/dot_general | solution.py:28
  291.4 31.3 %all-gather.1 = f32[131072]{0:T(1024)S(1)} all-gather(f32[16384]{0:T(1024)S(1)} %bitcast.18), channel_id=3, replica_groups=mesh['rows'=8,'code'=4] {'rows'}, dimensions={0}, use_global_device_ids=true | all-gather | bytes 589824 | tf_op jit(solution)/shard_map/all_gather | solution.py:29
  322.7 0.1 reshape.11
  322.8 0.1 reduce_sum.37
  323.0 26.2 %convolution_reduce_fusion.1 = f32[384]{0:T(512)S(1)} fusion(f32[16384,1]{0,1:T(1,128)S(1)} %bitcast.21, f32[384,16384]{1,0:T(8,128)} %get-tuple-element.5, f32[384]{0:T(512)S(1)} %pmax.7), kind=kOutput, calls=%fused_computation.10 | convolution fusion | flops 81788928 | bytes 25234432 | tf_op jit(solution)/shard_map/dot_general | solution.py:23
  349.2 5.9 psum.30
  355.1 18.0 %fusion.8 = f32[1,16384]{1,0:T(1,128)S(1)} fusion(f32[384,1]{0,1:T(1,128)S(1)} %reshape.23, f32[384,16384]{1,0:T(8,128)} %get-tuple-element.5, f32[384]{0:T(512)S(1)} %pmax.7), kind=kOutput, calls=%fused_computation.19 | convolution fusion | flops 81788928 | bytes 25234432 | tf_op jit(solution)/shard_map/dot_general | solution.py:28
  373.1 31.4 %all-gather.2 = f32[131072]{0:T(1024)S(1)} all-gather(f32[16384]{0:T(1024)S(1)} %bitcast.19), channel_id=4, replica_groups=mesh['rows'=8,'code'=4] {'rows'}, dimensions={0}, use_global_device_ids=true | all-gather | bytes 589824 | tf_op jit(solution)/shard_map/all_gather | solution.py:29
  404.5 0.1 reshape.12
  404.6 0.1 reduce_sum.38
  404.8 26.2 %convolution_reduce_fusion = f32[384]{0:T(512)S(1)} fusion(f32[16384,1]{0,1:T(1,128)S(1)} %bitcast.16, f32[384,16384]{1,0:T(8,128)} %get-tuple-element.5, f32[384]{0:T(512)S(1)} %pmax.7), kind=kOutput, calls=%fused_computation.9 | convolution fusion | flops 81788928 | bytes 25234432 | tf_op jit(solution)/shard_map/dot_general | solution.py:23
  431.0 5.7 psum.31
  436.6 11.9 %fusion.1 = f32[16384]{0:T(1024)} fusion(f32[16384]{0:T(1024)S(1)} %broadcast_divide_fusion, f32[384]{0:T(512)S(1)} %div.43, f32[384,16384]{1,0:T(8,128)} %get-tuple-element.5, f32[384]{0:T(512)S(1)} %pmax.7), kind=kLoop, calls=%fused_computation.4 | loop fusion | flops 25149440 | bytes 25299968 | tf_op jit(solution)/shard_map/reduce_sum | solution.py:32
  448.6 0.0 all-reduce.3.cloned.1.call-update
  448.6 0.0 copy-start.3
  448.6 0.0 copy-start.1
  448.6 0.3 reduce-scatter.2.cloned.1.call-start
  448.9 14.9 %fusion.2 = f32[16384,256]{1,0:T(8,128)} fusion(bf16[384,256]{1,0:T(8,128)(2,1)S(1)} %copy-done, f32[16384]{0:T(1024)S(1)} %broadcast_divide_fusion, f32[384]{0:T(512)S(1)} %div.43, f32[384,16384]{1,0:T(8,128)} %get-tuple-element.5, f32[384]{0:T(512)S(1)} %pmax.7), kind=kOutput, calls=%fused_computation.5 | convolution fusion | flops 3246391296 | bytes 42208256 | tf_op jit(solution)/shard_map/nk,nd->kd/dot_general | solution.py:33
  463.9 0.0 reduce-scatter.2.cloned.1.call-update
  463.9 0.0 copy-done.3
  463.9 0.6 dynamic-slice
  465.1 50.3 %all-reduce.3.cloned.1.call-done = f32[16384]{0:T(1024)} async-done(((f32[16384]{0:T(1024)}), f32[16384]{0:T(1024)}) %all-reduce.3.cloned.1.call-update) | async-done | bytes 65552
  515.4 1.3 broadcast_multiply_fusion
  516.7 285.0 %reduce-scatter.2.cloned.1.call-done = f32[2048,256]{1,0:T(8,128)} async-done(((f32[16384,256]{1,0:T(8,128)}), f32[2048,256]{1,0:T(8,128)}) %reduce-scatter.2.cloned.1.call-update) | async-done | bytes 2097168 | tf_op jit(solution)/shard_map/reduce_scatter | solution.py:40
  801.7 0.0 copy-done.1
  801.7 3.3 subtract_multiply_fusion
  (10 shorter events, 0.1 us)
Async XLA Ops:
  7.2 130.6 %copy-start = (bf16[384,256]{1,0:T(8,128)(2,1)S(1)}, bf16[384,256]{1,0:T(8,128)(2,1)}, u32[]{:S(2)}) copy-start(bf16[384,256]{1,0:T(8,128)(2,1)} %param.3) | copy-start | bytes 589828
  7.2 130.6 %all-gather.5.cloned.1.call-start = ((), (), s32[]{:S(2)}) async-start(), calls=%async_computation.1 | async-start | bytes 9437184 | tf_op jit(solution)/shard_map/all_gather | solution.py:16
  7.9 183.9 %copy-start.2 = (f32[384]{0:T(512)S(1)}, f32[384]{0:T(512)}, u32[]{:S(2)}) copy-start(f32[384]{0:T(512)} %param.5) | copy-start | bytes 4612
  7.9 507.5 %all-reduce.3.cloned.1.call-start = ((), (), s32[]{:S(2)}) async-start(), calls=%async_computation.3 | async-start | bytes 131072
  448.6 15.3 %copy-start.3 = (u32[32]{0:T(128)S(1)}, u32[32]{0:T(128)}, u32[]{:S(2)}) copy-start(u32[32]{0:T(128)} %constant.17) | copy-start | bytes 388
  448.6 353.1 %copy-start.1 = (bf16[2048,256]{1,0:T(8,128)(2,1)S(1)}, bf16[2048,256]{1,0:T(8,128)(2,1)}, u32[]{:S(2)}) copy-start(bf16[2048,256]{1,0:T(8,128)(2,1)} %param.4) | copy-start | bytes 3145732
  448.6 353.1 %reduce-scatter.2.cloned.1.call-start = ((), (), s32[]{:S(2)}) async-start(), calls=%async_computation.2 | async-start | bytes 18874368 | tf_op jit(solution)/shard_map/reduce_scatter | solution.py:40
Sparse Core Ops, SparseCore 0:
  10.1 127.6 all-gather.4
  448.7 66.6 all-reduce.2
  519.2 282.4 reduce-scatter.1
